TPU v7x, 256 devices: a whole 4x4x8 slice. The times are simulated.
256 devices in a mesh: seq: 64 (over z, x, core), tp: 4 (over y).
Axes of the slice: x: 4, y: 4, z: 8, core: 2. Of those that a mesh axis runs over, the one named last changes fastest.
Arguments:
- hidden: bfloat16 [32768, 4096], P(('seq', 'tp')), may hold values from -640 to 640
- norm_gain: float32 [4096], replicated, may hold values from 0.5 to 1.5
- w_query: bfloat16 [4096, 2048], P(None, 'tp'), may hold values from -0.078125 to 0.078125
- w_key: bfloat16 [4096, 1024], P(None, 'tp'), may hold values from -2.421875 to 2.421875
- w_value: bfloat16 [4096, 1024], P(None, 'tp'), may hold values from -0.09375 to 0.09375
- doc_start: int32 [32768], P('seq'), may hold values from 0 to 32767, as said below
- block_owner: int32 [1024], P('seq'), may hold values from 0 to 63, as said below
Outputs:
- context_rows: bfloat16 [32768, 2048], P(('seq', 'tp'))
- key_cache: bfloat16 [49152, 1024], P('seq', 'tp')
- value_cache: bfloat16 [49152, 1024], P('seq', 'tp')
Inputs may be any that keep to these rules, and one draw needn't show every extreme that they name: `doc_start`: rows with equal values form one document: consecutive rows beginning at the row whose number is that value. Every document has at most 256 rows and one has exactly 256; all but the last have at least 64. `block_owner`: owner numbers never fall along the blocks. Owner o holds the blocks from o * 16 + e(o) up to (o + 1) * 16 + e(o + 1) - 1, where -4 <= e <= 4 and e is 0 at both ends of the axis; so an owner holds between 8 and 24 blocks, and some owner holds exactly 24.
All inputs are finite; a program needn't handle non-finite values.
Results may differ from a plain program's by a relative error of at most 0.0078.
Values may be sent and summed in bfloat16 or wider, within the bound.
No kernel may reach another device: no remote copies, remote signals or barrier semaphores. Data moves between devices by JAX's collectives and lax.ppermute only.
A program may use at most 128 MiB of HBM per device.

v0:
```python
import jax
import jax.numpy as jnp
from jax import lax
from jax.sharding import PartitionSpec as P

HD = 128
DOC_MAX = 256
EPS = 1e-05
ROPE_BASE = 500000.0


def from_behind(array, axis, by):
    length = lax.axis_size(axis)
    pairs = [(i, i + by) for i in range(length) if 0 <= i + by < length]
    return lax.ppermute(array, axis, pairs)


def rotate(packed, positions, head_count):
    row_count = packed.shape[0]
    head_width = packed.shape[1] // head_count
    half_width = head_width // 2
    frequency = jnp.power(
        ROPE_BASE, -jnp.arange(half_width, dtype=jnp.float32) * (2.0 / head_width)
    )
    angles = positions.astype(jnp.float32)[:, None] * frequency[None, :]
    cosine = jnp.cos(angles)[:, None, :]
    sine_part = jnp.sin(angles)[:, None, :]
    reshaped = packed.reshape(row_count, head_count, head_width)
    first_half = reshaped[:, :, :half_width]
    second = reshaped[:, :, half_width:]
    rotated = jnp.concatenate(
        [first_half * cosine - second * sine_part, second * cosine + first_half * sine_part], axis=2
    )
    return rotated.reshape(row_count, head_count * head_width)


def project(rows_in, norm_gain, w_query, w_key, w_value, positions):
    widened = rows_in.astype(jnp.float32)
    inverse_rms = lax.rsqrt(jnp.mean(widened * widened, axis=1, keepdims=True) + EPS)
    normed = (widened * inverse_rms * norm_gain[None, :]).astype(jnp.bfloat16)
    queries = jnp.dot(normed, w_query, preferred_element_type=jnp.float32)
    keys_f = jnp.dot(normed, w_key, preferred_element_type=jnp.float32)
    values_f = jnp.dot(normed, w_value, preferred_element_type=jnp.float32)
    queries = rotate(queries, positions, queries.shape[1] // HD).astype(jnp.bfloat16)
    keys_f = rotate(keys_f, positions, keys_f.shape[1] // HD).astype(jnp.bfloat16)
    return (queries, keys_f, values_f.astype(jnp.bfloat16))


def attend(
    queries, keys_in, values_in, query_doc, query_row, key_doc, key_row, key_live, offset, reach
):
    row_count = queries.shape[0]
    groups = keys_in.shape[1] // HD
    per_group = queries.shape[1] // keys_in.shape[1]
    window = row_count + reach

    def one_tile(index):
        first = index * row_count
        key_first = first + offset - reach
        near_keys = lax.dynamic_slice_in_dim(keys_in, key_first, window, 0)
        near_values = lax.dynamic_slice_in_dim(values_in, key_first, window, 0)
        near_doc = lax.dynamic_slice_in_dim(key_doc, key_first, window, 0)
        near_row = lax.dynamic_slice_in_dim(key_row, key_first, window, 0)
        near_live = lax.dynamic_slice_in_dim(key_live, key_first, window, 0)
        query_four = queries.reshape(row_count, groups, per_group, HD)
        key_three = near_keys.reshape(window, groups, HD)
        value_three = near_values.reshape(window, groups, HD)
        scores = jnp.einsum(
            "rgjd,kgd->gjrk", query_four, key_three, preferred_element_type=jnp.float32
        ) * HD ** (-0.5)
        allowed = (
            (query_doc[:, None] == near_doc[None, :])
            & (near_row[None, :] <= query_row[:, None])
            & (near_live[None, :] > 0)
        )
        allowed = allowed | (jnp.arange(window)[None, :] == jnp.arange(row_count)[:, None] + reach)
        scores = jnp.where(allowed[None, None], scores, -jnp.inf)
        highest = jnp.max(scores, axis=3, keepdims=True)
        weights = jnp.exp(scores - highest)
        weights = (weights / jnp.sum(weights, axis=3, keepdims=True)).astype(jnp.bfloat16)
        blended = jnp.einsum(
            "gjrk,kgd->rgjd", weights, value_three, preferred_element_type=jnp.float32
        )
        return blended.astype(jnp.bfloat16).reshape(row_count, groups * per_group * HD)

    tiles = lax.map(one_tile, jnp.arange(row_count // row_count, dtype=jnp.int32))
    return tiles.reshape(row_count, queries.shape[1])


def shards(hidden, norm_gain, w_query, w_key, w_value, doc_start, block_owner):
    home_hidden = lax.all_gather(hidden, "tp", axis=0, tiled=True)
    my_index = lax.axis_index("seq")
    home_rows = home_hidden.shape[0]
    home_blocks = block_owner.shape[0]
    block_rows = home_rows // home_blocks
    spill_rows = home_blocks // 4 * block_rows
    frame_size = home_rows + 2 * spill_rows
    all_rows = lax.axis_size("seq") * home_rows
    row_number = my_index * home_rows + jnp.arange(home_rows, dtype=jnp.int32)
    row_owner = jnp.repeat(block_owner, block_rows)
    frame_number = my_index * home_rows - spill_rows + jnp.arange(frame_size, dtype=jnp.int32)
    queries, keys_own, values_own = project(
        home_hidden, norm_gain, w_query, w_key, w_value, row_number - doc_start
    )
    left = from_behind((keys_own, values_own, doc_start), "seq", 1)
    left_live = jnp.ones((home_rows,), jnp.int32) * (my_index > 0).astype(jnp.int32)
    home_context = attend(
        queries,
        jnp.concatenate([left[0], keys_own], axis=0),
        jnp.concatenate([left[1], values_own], axis=0),
        doc_start,
        row_number,
        jnp.concatenate([left[2], doc_start], axis=0),
        jnp.concatenate([row_number - home_rows, row_number], axis=0),
        jnp.concatenate([left_live, jnp.ones((home_rows,), jnp.int32)], axis=0),
        home_rows,
        DOC_MAX,
    )
    arrived = []
    for direction in (1, -1):
        low_row = home_rows - spill_rows if direction == 1 else 0
        payload = (
            keys_own[low_row : low_row + spill_rows],
            values_own[low_row : low_row + spill_rows],
            row_owner[low_row : low_row + spill_rows],
        )
        arrived.append(from_behind((payload[0], payload[1], payload[2]), "seq", direction))
    from_left, from_right = arrived
    frame_keys = jnp.concatenate([from_left[0], keys_own, from_right[0]], axis=0)
    frame_values = jnp.concatenate([from_left[1], values_own, from_right[1]], axis=0)
    frame_owner = jnp.concatenate([from_left[2], row_owner, from_right[2]], axis=0)
    frame_live = (
        (frame_owner == my_index) & (frame_number >= 0) & (frame_number < all_rows)
    ).astype(jnp.int32)
    live_column = frame_live[:, None] > 0
    key_cache = jnp.where(live_column, frame_keys, jnp.zeros((), jnp.bfloat16))
    value_cache = jnp.where(live_column, frame_values, jnp.zeros((), jnp.bfloat16))
    context_rows = lax.all_to_all(home_context, "tp", split_axis=0, concat_axis=1, tiled=True)
    return (context_rows, key_cache, value_cache)


def solution(mesh):
    return jax.shard_map(
        shards,
        mesh=mesh,
        in_specs=(
            P(("seq", "tp"), None),
            P(),
            P(None, "tp"),
            P(None, "tp"),
            P(None, "tp"),
            P("seq"),
            P("seq"),
        ),
        out_specs=(P(("seq", "tp"), None), P("seq", "tp"), P("seq", "tp")),
        check_vma=False,
    )
```

profile of v0, /device:TPU:128, one launch (start us, length us, event | category | flops | bytes accessed | tf_op | source)
XLA Modules:
  0.0 141.9 jit_solution(14735143676403520581)
XLA Ops:
  8.9 3.6 %collective-permute-start.4 = (s32[128]{0:T(128)S(1)}, s32[128]{0:T(128)S(1)}, u32[]{:S(2)}, u32[]{:S(2)}) collective-permute-start(s32[128]{0:T(128)S(1)} %slice.56), channel_id=1, source_target_pairs={{4,0},{8,4},{12,8},{16,12},{20,16},{24,20},{28,24},{32,28},{36,32}... | collective-permute-start | bytes 1544 | tf_op jit(solution)/shard_map/ppermute | solution.py:15
  12.7 1.9 %collective-permute-start.3 = (s32[128]{0:T(128)S(1)}, s32[128]{0:T(128)S(1)}, u32[]{:S(2)}, u32[]{:S(2)}) collective-permute-start(s32[128]{0:T(128)S(1)} %slice.54), channel_id=1, source_target_pairs={{0,4},{4,8},{8,12},{12,16},{16,20},{20,24},{24,28},{28,32},{32,36}... | collective-permute-start | bytes 1544 | tf_op jit(solution)/shard_map/ppermute | solution.py:15
  14.6 1.9 %collective-permute-start.1 = (s32[512]{0:T(512)}, s32[512]{0:T(512)S(1)}, u32[]{:S(2)}, u32[]{:S(2)}) collective-permute-start(s32[512]{0:T(512)} %param.12), channel_id=1, source_target_pairs={{0,4},{4,8},{8,12},{12,16},{16,20},{20,24},{24,28},{28,32},{32,36}... | collective-permute-start | bytes 6152 | tf_op jit(solution)/shard_map/ppermute | solution.py:15
  20.9 2.1 %collective-permute-done.1 = s32[512]{0:T(512)S(1)} collective-permute-done((s32[512]{0:T(512)}, s32[512]{0:T(512)S(1)}, u32[]{:S(2)}, u32[]{:S(2)}) %collective-permute-start.1) | collective-permute-done | bytes 2080 | tf_op jit(solution)/shard_map/ppermute | solution.py:15
  23.8 2.2 %fusion.9 = pred[512,768]{0,1:T(8,128)(4,1)} fusion(s32[512]{0:T(512)S(1)} %iota_add_fusion.1, s32[512]{0:T(512)S(1)} %get-tuple-element.62, s32[512]{0:T(512)} %param.12, s32[768]{0:T(1024)S(1)} %dynamic_slice.25, s32[768]{0:T(1024)S(1)} %dynamic_slice.24, pred[768]{0:T(1024)(128)(4,1)S(1)} %slice_compare_fusion), kind=kLoop, calls=%fused_computation.15 | loop fusion | flops 2359296 | bytes 406272 | tf_op jit(solution)/shard_map/while/body/eval_jaxpr/or | solution.py:76
  25.9 36.2 %all-gather.2.cloned.1.call-done = bf16[512,4096]{1,0:T(8,128)(2,1)} async-done(((bf16[128,4096]{1,0:T(8,128)(2,1)}), bf16[512,4096]{1,0:T(8,128)(2,1)}) %all-gather.2.cloned.1.call-update) | async-done | bytes 4194320 | tf_op jit(solution)/shard_map/all_gather | solution.py:91
  62.1 3.2 %fusion.1 = f32[512]{0:T(512)S(1)} fusion(bf16[512,4096]{1,0:T(8,128)(2,1)} %all-gather.2.cloned.1.call-done), kind=kLoop, calls=%fused_computation.3 | loop fusion | flops 6290944 | bytes 4196352 | tf_op jit(solution)/shard_map/reduce_sum | solution.py:39
  65.6 2.0 %convolution_convert_fusion = bf16[512,256]{1,0:T(8,128)(2,1)} fusion(bf16[4096,256]{1,0:T(8,128)(2,1)S(1)} %copy-done, bf16[512,4096]{1,0:T(8,128)(2,1)S(1)} %copy-done.1, f32[4096]{0:T(1024)S(1)} %copy-done.4, f32[512]{0:T(512)S(1)} %add_rsqrt_fusion), kind=kOutput, calls=%fused_computation.18 | convolution fusion | flops 1082261504 | bytes 6572032 | tf_op jit(solution)/shard_map/dot_general | solution.py:43
  68.5 1.9 %collective-permute-start = (bf16[512,256]{1,0:T(8,128)(2,1)}, bf16[512,256]{1,0:T(8,128)(2,1)}, u32[]{:S(2)}, u32[]{:S(2)}) collective-permute-start(bf16[512,256]{1,0:T(8,128)(2,1)} %convolution_convert_fusion), channel_id=1, source_target_pairs={{0,4},{4,8},{8,12},{12,16},{16,20},{20,24},{24,28},{28,32},{32,36}... | collective-permute-start | bytes 786440 | tf_op jit(solution)/shard_map/ppermute | solution.py:15
  70.5 3.5 %collective-permute-start.7 = (bf16[128,256]{1,0:T(8,128)(2,1)S(1)}, bf16[128,256]{1,0:T(8,128)(2,1)}, u32[]{:S(2)}, u32[]{:S(2)}) collective-permute-start(bf16[128,256]{1,0:T(8,128)(2,1)S(1)} %get-tuple-element.49), channel_id=1, source_target_pairs={{0,4},{4,8},{8,12},{12,16},{16,20},{20,24},{24,28},{28,32},{32,36}... | collective-permute-start | bytes 196616 | tf_op jit(solution)/shard_map/ppermute | solution.py:15
  73.9 5.4 %collective-permute-start.8 = (bf16[128,256]{1,0:T(8,128)(2,1)S(1)}, bf16[128,256]{1,0:T(8,128)(2,1)}, u32[]{:S(2)}, u32[]{:S(2)}) collective-permute-start(bf16[128,256]{1,0:T(8,128)(2,1)S(1)} %get-tuple-element.50), channel_id=1, source_target_pairs={{4,0},{8,4},{12,8},{16,12},{20,16},{24,20},{28,24},{32,28},{36,32}... | collective-permute-start | bytes 196616 | tf_op jit(solution)/shard_map/ppermute | solution.py:15
  79.4 1.6 %fusion.30 = f32[512,256]{0,1:T(8,128)S(1)} fusion(bf16[4096,256]{1,0:T(8,128)(2,1)S(1)} %copy-done.3, bf16[512,4096]{1,0:T(8,128)(2,1)S(1)} %copy-done.1, f32[4096]{0:T(1024)S(1)} %copy-done.4, f32[512]{0:T(512)S(1)} %add_rsqrt_fusion), kind=kOutput, calls=%fused_computation.59 | convolution fusion | flops 1082130432 | bytes 6834176 | tf_op jit(solution)/shard_map/dot_general | solution.py:42
  82.0 1.2 copy.45
  83.2 1.6 %subtract_convert_fusion.1 = (bf16[512,2,64]{2,1,0:T(2,128)(2,1)S(1)}, bf16[512,2,64]{2,1,0:T(2,128)(2,1)S(1)}) fusion(f32[512,2,64]{2,1,0:T(2,128)S(1)} %copy.46, f32[512,2,64]{2,1,0:T(2,128)S(1)} %copy.45, f32[512,64]{1,0:T(8,128)} %copy.32, f32[512,64]{1,0:T(8,128)} %copy.30), kind=kLoop, calls=%fused_computation.24 | loop fusion | flops 524288 | bytes 1048576 | tf_op jit(solution)/shard_map/convert.2
  85.5 1.9 %collective-permute-start.2 = (bf16[512,256]{1,0:T(8,128)(2,1)S(1)}, bf16[512,256]{1,0:T(8,128)(2,1)S(1)}, u32[]{:S(2)}, u32[]{:S(2)}) collective-permute-start(bf16[512,256]{1,0:T(8,128)(2,1)S(1)} %bitcast.51), channel_id=1, source_target_pairs={{0,4},{4,8},{8,12},{12,16},{16,20},{20,24},{24,28},{28,32},{32,36}... | collective-permute-start | bytes 786440 | tf_op jit(solution)/shard_map/ppermute | solution.py:15
  87.4 5.9 %fusion.28 = f32[512,512]{0,1:T(8,128)S(1)} fusion(bf16[4096,512]{1,0:T(8,128)(2,1)} %param.9, bf16[512,4096]{1,0:T(8,128)(2,1)} %all-gather.2.cloned.1.call-done, f32[4096]{0:T(1024)} %param.8, f32[512]{0:T(512)S(1)} %add_rsqrt_fusion), kind=kOutput, calls=%fused_computation.58 | convolution fusion | flops 2155872256 | bytes 9455616 | tf_op jit(solution)/shard_map/dot_general | solution.py:41
  94.0 7.0 %collective-permute-start.6 = (bf16[128,256]{1,0:T(8,128)(2,1)S(1)}, bf16[128,256]{1,0:T(8,128)(2,1)S(1)}, u32[]{:S(2)}, u32[]{:S(2)}) collective-permute-start(bf16[128,256]{1,0:T(8,128)(2,1)S(1)} %bitcast.60), channel_id=1, source_target_pairs={{4,0},{8,4},{12,8},{16,12},{20,16},{24,20},{28,24},{32,28},{36,32}... | collective-permute-start | bytes 196616 | tf_op jit(solution)/shard_map/ppermute | solution.py:15
  100.9 2.1 %collective-permute-start.5 = (bf16[128,256]{1,0:T(8,128)(2,1)S(1)}, bf16[128,256]{1,0:T(8,128)(2,1)S(1)}, u32[]{:S(2)}, u32[]{:S(2)}) collective-permute-start(bf16[128,256]{1,0:T(8,128)(2,1)S(1)} %bitcast.59), channel_id=1, source_target_pairs={{0,4},{4,8},{8,12},{12,16},{16,20},{20,24},{24,28},{28,32},{32,36}... | collective-permute-start | bytes 196616 | tf_op jit(solution)/shard_map/ppermute | solution.py:15
  103.1 6.7 %collective-permute-done.5 = bf16[128,256]{1,0:T(8,128)(2,1)S(1)} collective-permute-done((bf16[128,256]{1,0:T(8,128)(2,1)S(1)}, bf16[128,256]{1,0:T(8,128)(2,1)S(1)}, u32[]{:S(2)}, u32[]{:S(2)}) %collective-permute-start.5) | collective-permute-done | bytes 65568 | tf_op jit(solution)/shard_map/ppermute | solution.py:15
  109.9 2.3 %maximum_select_fusion.1 = (bf16[768,256]{1,0:T(8,128)(2,1)}, bf16[768,256]{1,0:T(8,128)(2,1)S(1)}, bf16[768,256]{1,0:T(8,128)(2,1)S(1)}, bf16[768,256]{1,0:T(8,128)(2,1)}) fusion(bf16[128,256]{1,0:T(8,128)(2,1)} %collective-permute-done.8, bf16[512,256]{1,0:T(8,128)(2,1)} %convolution_convert_fusion, bf16[128,256]{1,0:T(8,128)(2,1)} %collective-permute-done.7, ...), kind=kLoop, calls=%fused_computation.28 | loop fusion | flops 4325376 | bytes 2884352 | tf_op jit(solution)/shard_map/jit(_where)/select_n | solution.py:137
  113.2 6.1 %fusion.36 = (f32[2,2,512]{2,1,0:T(2,128)S(1)}, f32[2,2,512,768]{2,3,1,0:T(8,128)}) fusion(pred[512,768]{0,1:T(8,128)(4,1)} %fusion.9, bf16[512,2,2,128]{0,3,2,1:T(8,128)(2,1)S(1)} %bitcast.53, bf16[768,2,128,1]{2,1,0,3:T(2,128)(2,1)S(1)} %bitcast.56), kind=kOutput, calls=%fused_computation.63 | convolution fusion | flops 408945408 | bytes 7610368 | tf_op jit(solution)/shard_map/while/body/eval_jaxpr/sub | solution.py:79
  119.3 3.4 %fusion.11 = bf16[512,2,2,128]{0,3,2,1:T(8,128)(2,1)S(1)} fusion(bf16[768,2,128,1]{0,2,3,1:T(8,128)(2,1)S(1)} %bitcast.55, f32[2,2,512,768]{2,3,1,0:T(8,128)} %get-tuple-element.60, f32[2,2,512]{2,1,0:T(2,128)S(1)} %get-tuple-element.59), kind=kOutput, calls=%fused_computation.17 | convolution fusion | flops 406061056 | bytes 7217152 | tf_op jit(solution)/shard_map/while/body/eval_jaxpr/gjrk,kgd->rgjd/dot_general | solution.py:81
  122.9 11.2 %all_to_all.19 = bf16[4,128,512]{1,2,0:T(8,128)(2,1)S(1)} all-to-all(bf16[4,128,512]{1,2,0:T(8,128)(2,1)S(1)} %copy.37), channel_id=1, replica_groups=mesh['seq'=64,'tp'=4] {'tp'}, dimensions={0} | all-to-all | bytes 1048576 | tf_op jit(solution)/shard_map/all_to_all | solution.py:138
  134.1 1.0 copy.38
  (55 shorter events, 11.5 us)
Async XLA Ops:
  7.2 58.2 %copy-start = (bf16[4096,256]{1,0:T(8,128)(2,1)S(1)}, bf16[4096,256]{1,0:T(8,128)(2,1)}, u32[]{:S(2)}) copy-start(bf16[4096,256]{1,0:T(8,128)(2,1)} %param.11) | copy-start | bytes 6291460
  7.2 58.2 %copy-start.4 = (f32[4096]{0:T(1024)S(1)}, f32[4096]{0:T(1024)}, u32[]{:S(2)}) copy-start(f32[4096]{0:T(1024)} %param.8) | copy-start | bytes 49156
  7.2 54.9 %all-gather.2.cloned.1.call-start = ((), (), s32[]{:S(2)}) async-start(), calls=%async_computation.1 | async-start | bytes 5242880 | tf_op jit(solution)/shard_map/all_gather | solution.py:91
  8.9 11.4 %collective-permute-start.4 = (s32[128]{0:T(128)S(1)}, s32[128]{0:T(128)S(1)}, u32[]{:S(2)}, u32[]{:S(2)}) collective-permute-start(s32[128]{0:T(128)S(1)} %slice.56), channel_id=1, source_target_pairs={{4,0},{8,4},{12,8},{16,12},{20,16},{24,20},{28,24},{32,28},{36,32}... | collective-permute-start | bytes 1544 | tf_op jit(solution)/shard_map/ppermute | solution.py:15
  12.7 8.2 %collective-permute-start.3 = (s32[128]{0:T(128)S(1)}, s32[128]{0:T(128)S(1)}, u32[]{:S(2)}, u32[]{:S(2)}) collective-permute-start(s32[128]{0:T(128)S(1)} %slice.54), channel_id=1, source_target_pairs={{0,4},{4,8},{8,12},{12,16},{16,20},{20,24},{24,28},{28,32},{32,36}... | collective-permute-start | bytes 1544 | tf_op jit(solution)/shard_map/ppermute | solution.py:15
  14.6 8.4 %collective-permute-start.1 = (s32[512]{0:T(512)}, s32[512]{0:T(512)S(1)}, u32[]{:S(2)}, u32[]{:S(2)}) collective-permute-start(s32[512]{0:T(512)} %param.12), channel_id=1, source_target_pairs={{0,4},{4,8},{8,12},{12,16},{16,20},{20,24},{24,28},{28,32},{32,36}... | collective-permute-start | bytes 6152 | tf_op jit(solution)/shard_map/ppermute | solution.py:15
  62.1 3.4 %copy-start.1 = (bf16[512,4096]{1,0:T(8,128)(2,1)S(1)}, bf16[512,4096]{1,0:T(8,128)(2,1)}, u32[]{:S(2)}) copy-start(bf16[512,4096]{1,0:T(8,128)(2,1)} %all-gather.2.cloned.1.call-done) | copy-start | bytes 12582916
  65.6 13.8 %copy-start.3 = (bf16[4096,256]{1,0:T(8,128)(2,1)S(1)}, bf16[4096,256]{1,0:T(8,128)(2,1)}, u32[]{:S(2)}) copy-start(bf16[4096,256]{1,0:T(8,128)(2,1)} %param.10) | copy-start | bytes 6291460
  68.5 41.3 %collective-permute-start = (bf16[512,256]{1,0:T(8,128)(2,1)}, bf16[512,256]{1,0:T(8,128)(2,1)}, u32[]{:S(2)}, u32[]{:S(2)}) collective-permute-start(bf16[512,256]{1,0:T(8,128)(2,1)} %convolution_convert_fusion), channel_id=1, source_target_pairs={{0,4},{4,8},{8,12},{12,16},{16,20},{20,24},{24,28},{28,32},{32,36}... | collective-permute-start | bytes 786440 | tf_op jit(solution)/shard_map/ppermute | solution.py:15
  70.5 30.5 %collective-permute-start.7 = (bf16[128,256]{1,0:T(8,128)(2,1)S(1)}, bf16[128,256]{1,0:T(8,128)(2,1)}, u32[]{:S(2)}, u32[]{:S(2)}) collective-permute-start(bf16[128,256]{1,0:T(8,128)(2,1)S(1)} %get-tuple-element.49), channel_id=1, source_target_pairs={{0,4},{4,8},{8,12},{12,16},{16,20},{20,24},{24,28},{28,32},{32,36}... | collective-permute-start | bytes 196616 | tf_op jit(solution)/shard_map/ppermute | solution.py:15
  73.9 29.2 %collective-permute-start.8 = (bf16[128,256]{1,0:T(8,128)(2,1)S(1)}, bf16[128,256]{1,0:T(8,128)(2,1)}, u32[]{:S(2)}, u32[]{:S(2)}) collective-permute-start(bf16[128,256]{1,0:T(8,128)(2,1)S(1)} %get-tuple-element.50), channel_id=1, source_target_pairs={{4,0},{8,4},{12,8},{16,12},{20,16},{24,20},{28,24},{32,28},{36,32}... | collective-permute-start | bytes 196616 | tf_op jit(solution)/shard_map/ppermute | solution.py:15
  85.5 24.4 %collective-permute-start.2 = (bf16[512,256]{1,0:T(8,128)(2,1)S(1)}, bf16[512,256]{1,0:T(8,128)(2,1)S(1)}, u32[]{:S(2)}, u32[]{:S(2)}) collective-permute-start(bf16[512,256]{1,0:T(8,128)(2,1)S(1)} %bitcast.51), channel_id=1, source_target_pairs={{0,4},{4,8},{8,12},{12,16},{16,20},{20,24},{24,28},{28,32},{32,36}... | collective-permute-start | bytes 786440 | tf_op jit(solution)/shard_map/ppermute | solution.py:15
  94.0 9.1 %collective-permute-start.6 = (bf16[128,256]{1,0:T(8,128)(2,1)S(1)}, bf16[128,256]{1,0:T(8,128)(2,1)S(1)}, u32[]{:S(2)}, u32[]{:S(2)}) collective-permute-start(bf16[128,256]{1,0:T(8,128)(2,1)S(1)} %bitcast.60), channel_id=1, source_target_pairs={{4,0},{8,4},{12,8},{16,12},{20,16},{24,20},{28,24},{32,28},{36,32}... | collective-permute-start | bytes 196616 | tf_op jit(solution)/shard_map/ppermute | solution.py:15
  100.9 8.9 %collective-permute-start.5 = (bf16[128,256]{1,0:T(8,128)(2,1)S(1)}, bf16[128,256]{1,0:T(8,128)(2,1)S(1)}, u32[]{:S(2)}, u32[]{:S(2)}) collective-permute-start(bf16[128,256]{1,0:T(8,128)(2,1)S(1)} %bitcast.59), channel_id=1, source_target_pairs={{0,4},{4,8},{8,12},{12,16},{16,20},{20,24},{24,28},{28,32},{32,36}... | collective-permute-start | bytes 196616 | tf_op jit(solution)/shard_map/ppermute | solution.py:15
  113.2 6.1 %copy-start.2 = (bf16[768,256]{0,1:T(8,128)(2,1)S(1)}, bf16[768,256]{0,1:T(8,128)(2,1)}, u32[]{:S(2)}) copy-start(bf16[768,256]{0,1:T(8,128)(2,1)} %copy.42) | copy-start | bytes 1179652
Sparse Core Ops, SparseCore 0:
  9.8 52.2 all-gather.1
where the time goes:
time: 143 us; the launch traced here: 142 us
  waiting for transfers between devices  46.3 us (32%)
  starting transfers between devices  29.3 us (20%)
  matrix products  19.1 us (13%)
  between operations  14.4 us (10%)
  other arithmetic  12.5 us (9%)
  blocking collectives  11.2 us (8%)
  local copies, waits for them, and re-layouts  9.14 us (6%)
    all_gather x1, waiting for transfers between devices, shards(): home_hidden = lax.all_gather(hidden, 'tp', axis=0, tiled=True)  36.2 us
    ppermute x9, starting transfers between devices, from_behind(): return lax.ppermute(array, axis, pairs)  29.3 us
    all_to_all x1, blocking collectives, shards(): lax.all_to_all(home_context, 'tp', split_axis=0, concat_axis=1, tiled=True)  11.2 us
    ppermute x9, waiting for transfers between devices, from_behind(): return lax.ppermute(array, axis, pairs)  9.44 us
    sub x1, matrix products, one_tile(): weights = jnp.exp(scores - highest)  6.09 us
    dot_general x1, matrix products, project(): queries = jnp.dot(normed, w_query, preferred_element_type=jnp.float32)  5.94 us
    dot_general x1, matrix products, one_tile(): jnp.einsum('gjrk,kgd->rgjd', weights, value_three, preferred_element_type...  3.37 us
    reduce_sum x1, other arithmetic, project(): jnp.mean(widened * widened, axis=1, keepdims=True) + EPS  3.23 us
  transfers between devices with their start and end apart: 10, of which 4 were waited for; matrix products, arithmetic and copies ran while one was open for 14% of the time, Pallas kernels for 0%

commit v1 on v0

--- a/solution.py
+++ b/solution.py
@@ -2,6 +2,7 @@
 import jax.numpy as jnp
 from jax import lax
 from jax.sharding import PartitionSpec as P
+from jax.lax import all_to_all, axis_size
 
 HD = 128
 DOC_MAX = 256
@@ -88,7 +89,16 @@
 
 
 def shards(hidden, norm_gain, w_query, w_key, w_value, doc_start, block_owner):
-    home_hidden = lax.all_gather(hidden, "tp", axis=0, tiled=True)
+
+    def perform_plate_on_mesh(d_out, shard_in):
+        axis_id = "tp"
+        earlier = axis_size(axis_id)
+        block_next = jnp.concatenate([shard_in] * earlier, d_out)
+        return all_to_all(
+            block_next, split_axis=d_out, concat_axis=d_out, axis_name=axis_id, tiled=True
+        )
+
+    home_hidden = perform_plate_on_mesh(0, hidden)
     my_index = lax.axis_index("seq")
     home_rows = home_hidden.shape[0]
     home_blocks = block_owner.shape[0]

time: 143 us -> 133 us (0.930)
  between operations: 14.4 us -> 1 us
  waiting for transfers between devices: 46.3 us -> 34.4 us
  other arithmetic: 12.5 us -> 20.5 us
  local copies, waits for them, and re-layouts: 9.14 us -> 14.1 us
  starting transfers between devices: 29.3 us -> 34.2 us
    all_gather x1 -> x0, waiting for transfers between devices: 36.2 us -> none  [shards(): home_hidden = lax.all_gather(hidden, 'tp', axis=0, tiled=True)]
    all_to_all x0 -> x1, waiting for transfers between devices: none -> 28.4 us  [perform_plate_on_mesh(): all_to_all(block_next, split_axis=d_out, concat_axis=d_out, axis_name=axi...]
    dot_general x0 -> x2, local copies, waits for them, and re-layouts: none -> 10.5 us  [the longest x1 6.39 us: project(): queries = jnp.dot(normed, w_query, preferred_element_type=jnp.float32)]
    convert_element_type x0 -> x2, other arithmetic: none -> 7.79 us  [project(): normed = (widened * inverse_rms * norm_gain[None, :]).astype(jnp.bfloat16)]
    all_to_all x0 -> x1, starting transfers between devices: none -> 4.98 us  [perform_plate_on_mesh(): all_to_all(block_next, split_axis=d_out, concat_axis=d_out, axis_name=axi...]
    concatenate x0 -> x1, other arithmetic: none -> 4.24 us  [perform_plate_on_mesh(): block_next = jnp.concatenate([shard_in] * earlier, d_out)]
    ppermute x9, waiting for transfers between devices: 9.44 us -> 5.98 us  [from_behind(): return lax.ppermute(array, axis, pairs)]
    another operation x2, other arithmetic: 1.76 us -> 0.27 us
  transfers between devices with their start and end apart: 10 -> 10, of which waited for: 4 -> 2; matrix products, arithmetic and copies ran while one was open for 14% -> 19% of each run, Pallas kernels for 0% -> 0%
where the time goes in v1:
time: 133 us
  waiting for transfers between devices  34.4 us (26%)
  starting transfers between devices  34.2 us (26%)
  other arithmetic  20.5 us (15%)
  matrix products  17.9 us (13%)
  local copies, waits for them, and re-layouts  14.1 us (11%)
  blocking collectives  10.5 us (8%)
    ppermute x9, starting transfers between devices, from_behind(): return lax.ppermute(array, axis, pairs)  29.3 us
    all_to_all x1, waiting for transfers between devices, perform_plate_on_mesh(): all_to_all(block_next, split_axis=d_out, concat_axis=d_out, axis_name=axi...  28.4 us
    all_to_all x1, blocking collectives, shards(): lax.all_to_all(home_context, 'tp', split_axis=0, concat_axis=1, tiled=True)  10.5 us
    convert_element_type x2, other arithmetic, project(): normed = (widened * inverse_rms * norm_gain[None, :]).astype(jnp.bfloat16)  7.79 us
    dot_general x1, local copies, waits for them, and re-layouts, project(): queries = jnp.dot(normed, w_query, preferred_element_type=jnp.float32)  6.39 us
    sub x1, matrix products, one_tile(): weights = jnp.exp(scores - highest)  6.17 us
    ppermute x9, waiting for transfers between devices, from_behind(): return lax.ppermute(array, axis, pairs)  5.98 us
    dot_general x1, matrix products, project(): queries = jnp.dot(normed, w_query, preferred_element_type=jnp.float32)  5.82 us
  transfers between devices with their start and end apart: 10, of which 2 were waited for; matrix products, arithmetic and copies ran while one was open for 19% of the time, Pallas kernels for 0%

profile of v1, /device:TPU:128, one launch (start us, length us, event | category | flops | bytes accessed | tf_op | source)
XLA Modules:
  0.0 132.6 jit_solution(14283194901348656739)
XLA Ops:
  0.6 4.2 %pad_maximum_fusion = bf16[512,4096]{1,0:T(8,128)(2,1)} fusion(bf16[128,4096]{1,0:T(8,128)(2,1)} %param.7), kind=kLoop, calls=%fused_computation.10 | loop fusion | flops 16777216 | bytes 5242880 | tf_op jit(solution)/shard_map/concatenate | solution.py:96
  4.9 5.0 %all-to-all-start = ((bf16[4,128,4096]{2,1,0:T(8,128)(2,1)}), bf16[4,128,4096]{2,1,0:T(8,128)(2,1)}, u32[]{:S(2)}, u32[]{:S(2)}) async-start(bf16[4,128,4096]{2,1,0:T(8,128)(2,1)} %bitcast.55), calls=%async_computation | async-start | bytes 8388608 | tf_op jit(solution)/shard_map/all_to_all | solution.py:97
  10.1 3.6 %collective-permute-start.4 = (s32[128]{0:T(128)S(1)}, s32[128]{0:T(128)S(1)}, u32[]{:S(2)}, u32[]{:S(2)}) collective-permute-start(s32[128]{0:T(128)S(1)} %slice.56), channel_id=1, source_target_pairs={{4,0},{8,4},{12,8},{16,12},{20,16},{24,20},{28,24},{32,28},{36,32}... | collective-permute-start | bytes 1544 | tf_op jit(solution)/shard_map/ppermute | solution.py:16
  13.9 1.9 %collective-permute-start.3 = (s32[128]{0:T(128)S(1)}, s32[128]{0:T(128)S(1)}, u32[]{:S(2)}, u32[]{:S(2)}) collective-permute-start(s32[128]{0:T(128)S(1)} %slice.54), channel_id=1, source_target_pairs={{0,4},{4,8},{8,12},{12,16},{16,20},{20,24},{24,28},{28,32},{32,36}... | collective-permute-start | bytes 1544 | tf_op jit(solution)/shard_map/ppermute | solution.py:16
  15.9 1.9 %collective-permute-start.1 = (s32[512]{0:T(512)S(1)}, s32[512]{0:T(512)S(1)}, u32[]{:S(2)}, u32[]{:S(2)}) collective-permute-start(s32[512]{0:T(512)S(1)} %copy-done.4), channel_id=1, source_target_pairs={{0,4},{4,8},{8,12},{12,16},{16,20},{20,24},{24,28},{28,32},{32,36}... | collective-permute-start | bytes 6152 | tf_op jit(solution)/shard_map/ppermute | solution.py:16
  18.6 4.1 %copy.36 = bf16[256,4096]{1,0:T(8,128)(2,1)} copy(bf16[256,4096]{0,1:T(8,128)(2,1)} %bitcast.60) | data formatting | bytes 4194304 | tf_op jit(solution)/shard_map/dot_general | solution.py:43
  22.7 6.4 %copy.40 = bf16[512,4096]{1,0:T(8,128)(2,1)} copy(bf16[512,4096]{0,1:T(8,128)(2,1)} %bitcast.58) | data formatting | bytes 8388608 | tf_op jit(solution)/shard_map/dot_general | solution.py:42
  29.1 1.5 %fusion.8 = pred[512,768]{0,1:T(8,128)(4,1)} fusion(s32[512]{0:T(512)S(1)} %iota_add_fusion.1, s32[512]{0:T(512)S(1)} %get-tuple-element.59, s32[512]{0:T(512)S(1)} %copy-done.4, s32[768]{0:T(1024)S(1)} %dynamic_slice.25, s32[768]{0:T(1024)S(1)} %dynamic_slice.24, pred[768]{0:T(1024)(128)(4,1)S(1)} %slice_compare_fusion), kind=kLoop, calls=%fused_computation.16 | loop fusion | flops 2359296 | bytes 406272 | tf_op jit(solution)/shard_map/while/body/eval_jaxpr/or | solution.py:77
  30.6 28.4 %all-to-all-done = bf16[4,128,4096]{2,1,0:T(8,128)(2,1)} async-done(((bf16[4,128,4096]{2,1,0:T(8,128)(2,1)}), bf16[4,128,4096]{2,1,0:T(8,128)(2,1)}, u32[]{:S(2)}, u32[]{:S(2)}) %all-to-all-start) | async-done | bytes 4194336 | tf_op jit(solution)/shard_map/all_to_all | solution.py:97
  59.0 3.1 %multiply_reduce_fusion = f32[4,128]{1,0:T(4,128)S(1)} fusion(bf16[4,128,4096]{2,1,0:T(8,128)(2,1)} %all-to-all-done), kind=kLoop, calls=%fused_computation.5 | loop fusion | flops 6290944 | bytes 4196352 | tf_op jit(solution)/shard_map/reduce_sum | solution.py:40
  62.1 3.8 %fusion.2 = bf16[512,4096]{1,0:T(8,128)(2,1)S(1)} fusion(bf16[4,128,4096]{2,1,0:T(8,128)(2,1)} %all-to-all-done, f32[4096]{0:T(1024)S(1)} %copy-done.3, f32[512]{0:T(512)S(1)} %get-tuple-element.51), kind=kLoop, calls=%fused_computation.3 | loop fusion | flops 8388608 | bytes 8407040 | tf_op jit(solution)/shard_map/convert_element_type | solution.py:41
  67.9 1.9 %collective-permute-start = (bf16[512,256]{1,0:T(8,128)(2,1)S(1)}, bf16[512,256]{1,0:T(8,128)(2,1)}, u32[]{:S(2)}, u32[]{:S(2)}) collective-permute-start(bf16[512,256]{1,0:T(8,128)(2,1)S(1)} %convolution_convert_fusion), channel_id=1, source_target_pairs={{0,4},{4,8},{8,12},{12,16},{16,20},{20,24},{24,28},{28,32},{32,36}... | collective-permute-start | bytes 786440 | tf_op jit(solution)/shard_map/ppermute | solution.py:16
  69.8 4.0 %multiply_convert_fusion = bf16[4,128,4096]{2,1,0:T(8,128)(2,1)S(1)} fusion(bf16[4,128,4096]{2,1,0:T(8,128)(2,1)} %all-to-all-done, f32[4096]{0:T(1024)S(1)} %copy-done.3, f32[4,128]{1,0:T(4,128)S(1)} %get-tuple-element.50), kind=kLoop, calls=%fused_computation.4 | loop fusion | flops 8388608 | bytes 8407040 | tf_op jit(solution)/shard_map/convert_element_type | solution.py:41
  75.8 7.0 %collective-permute-start.8 = (bf16[128,256]{1,0:T(8,128)(2,1)}, bf16[128,256]{1,0:T(8,128)(2,1)}, u32[]{:S(2)}, u32[]{:S(2)}) collective-permute-start(bf16[128,256]{1,0:T(8,128)(2,1)} %get-tuple-element.43), channel_id=1, source_target_pairs={{4,0},{8,4},{12,8},{16,12},{20,16},{24,20},{28,24},{32,28},{36,32}... | collective-permute-start | bytes 196616 | tf_op jit(solution)/shard_map/ppermute | solution.py:16
  82.8 1.9 %collective-permute-start.7 = (bf16[128,256]{1,0:T(8,128)(2,1)}, bf16[128,256]{1,0:T(8,128)(2,1)}, u32[]{:S(2)}, u32[]{:S(2)}) collective-permute-start(bf16[128,256]{1,0:T(8,128)(2,1)} %get-tuple-element.42), channel_id=1, source_target_pairs={{0,4},{4,8},{8,12},{12,16},{16,20},{20,24},{24,28},{28,32},{32,36}... | collective-permute-start | bytes 196616 | tf_op jit(solution)/shard_map/ppermute | solution.py:16
  84.9 1.9 %collective-permute-start.2 = (bf16[512,256]{1,0:T(8,128)(2,1)S(1)}, bf16[512,256]{1,0:T(8,128)(2,1)}, u32[]{:S(2)}, u32[]{:S(2)}) collective-permute-start(bf16[512,256]{1,0:T(8,128)(2,1)S(1)} %copy.37), channel_id=1, source_target_pairs={{0,4},{4,8},{8,12},{12,16},{16,20},{20,24},{24,28},{28,32},{32,36}... | collective-permute-start | bytes 786440 | tf_op jit(solution)/shard_map/ppermute | solution.py:16
  86.9 7.0 %collective-permute-start.6 = (bf16[128,256]{1,0:T(8,128)(2,1)S(1)}, bf16[128,256]{1,0:T(8,128)(2,1)}, u32[]{:S(2)}, u32[]{:S(2)}) collective-permute-start(bf16[128,256]{1,0:T(8,128)(2,1)S(1)} %copy.42), channel_id=1, source_target_pairs={{4,0},{8,4},{12,8},{16,12},{20,16},{24,20},{28,24},{32,28},{36,32}... | collective-permute-start | bytes 196616 | tf_op jit(solution)/shard_map/ppermute | solution.py:16
  93.9 5.8 %fusion.38 = f32[512,4,128]{0,2,1:T(8,128)S(1)} fusion(bf16[512,4096,1]{1,0,2:T(8,128)(2,1)} %bitcast.57, bf16[4,128,4096]{2,1,0:T(8,128)(2,1)} %bitcast.59), kind=kOutput, calls=%fused_computation.65 | convolution fusion | flops 2147483648 | bytes 9437184 | tf_op jit(solution)/shard_map/dot_general | solution.py:42
  100.0 2.1 %collective-permute-start.5 = (bf16[128,256]{1,0:T(8,128)(2,1)S(1)}, bf16[128,256]{1,0:T(8,128)(2,1)S(1)}, u32[]{:S(2)}, u32[]{:S(2)}) collective-permute-start(bf16[128,256]{1,0:T(8,128)(2,1)S(1)} %copy.41), channel_id=1, source_target_pairs={{0,4},{4,8},{8,12},{12,16},{16,20},{20,24},{24,28},{28,32},{32,36}... | collective-permute-start | bytes 196616 | tf_op jit(solution)/shard_map/ppermute | solution.py:16
  103.0 6.0 %collective-permute-done.5 = bf16[128,256]{1,0:T(8,128)(2,1)S(1)} collective-permute-done((bf16[128,256]{1,0:T(8,128)(2,1)S(1)}, bf16[128,256]{1,0:T(8,128)(2,1)S(1)}, u32[]{:S(2)}, u32[]{:S(2)}) %collective-permute-start.5) | collective-permute-done | bytes 65568 | tf_op jit(solution)/shard_map/ppermute | solution.py:16
  108.9 2.2 %maximum_select_fusion.1 = (bf16[768,256]{1,0:T(8,128)(2,1)}, bf16[768,256]{1,0:T(8,128)(2,1)S(1)}, bf16[768,256]{1,0:T(8,128)(2,1)S(1)}, bf16[768,256]{1,0:T(8,128)(2,1)}) fusion(bf16[128,256]{1,0:T(8,128)(2,1)} %collective-permute-done.8, bf16[512,256]{1,0:T(8,128)(2,1)S(1)} %convolution_convert_fusion, bf16[128,256]{1,0:T(8,128)(2,1)} %collective-permute-done.7, ...), kind=kLoop, calls=%fused_computation.27 | loop fusion | flops 4325376 | bytes 2884352 | tf_op jit(solution)/shard_map/jit(_where)/select_n | solution.py:147
  111.4 6.2 %fusion.32 = (f32[2,2,512]{2,1,0:T(2,128)S(1)}, f32[2,2,512,768]{2,3,1,0:T(8,128)}) fusion(pred[512,768]{0,1:T(8,128)(4,1)} %fusion.8, bf16[512,2,2,128]{0,3,2,1:T(8,128)(2,1)} %bitcast.64, bf16[768,2,128,1]{2,1,0,3:T(2,128)(2,1)S(1)} %bitcast.66), kind=kOutput, calls=%fused_computation.63 | convolution fusion | flops 408945408 | bytes 7610368 | tf_op jit(solution)/shard_map/while/body/eval_jaxpr/sub | solution.py:80
  117.5 3.4 %fusion.10 = bf16[512,2,2,128]{0,3,2,1:T(8,128)(2,1)S(1)} fusion(bf16[768,2,128,1]{0,2,3,1:T(8,128)(2,1)S(1)} %bitcast.65, f32[2,2,512,768]{2,3,1,0:T(8,128)} %get-tuple-element.57, f32[2,2,512]{2,1,0:T(2,128)S(1)} %get-tuple-element.56), kind=kOutput, calls=%fused_computation.18 | convolution fusion | flops 406061056 | bytes 7217152 | tf_op jit(solution)/shard_map/while/body/eval_jaxpr/gjrk,kgd->rgjd/dot_general | solution.py:82
  121.1 10.5 %all_to_all.28 = bf16[4,128,512]{1,2,0:T(8,128)(2,1)S(1)} all-to-all(bf16[4,128,512]{1,2,0:T(8,128)(2,1)S(1)} %copy.27), channel_id=1, replica_groups=mesh['seq'=64,'tp'=4] {'tp'}, dimensions={0} | all-to-all | bytes 1048576 | tf_op jit(solution)/shard_map/all_to_all | solution.py:148
  (56 shorter events, 7.9 us)
Async XLA Ops:
  0.6 65.3 %copy-start = (bf16[4096,256]{1,0:T(8,128)(2,1)S(1)}, bf16[4096,256]{1,0:T(8,128)(2,1)}, u32[]{:S(2)}) copy-start(bf16[4096,256]{1,0:T(8,128)(2,1)} %param.11) | copy-start | bytes 6291460
  4.9 5.0 %copy-start.5 = (s32[16]{0:T(128)S(1)}, s32[16]{0:T(128)}, u32[]{:S(2)}) copy-start(s32[16]{0:T(128)} %param.13) | copy-start | bytes 196
  4.9 11.0 %copy-start.4 = (s32[512]{0:T(512)S(1)}, s32[512]{0:T(512)}, u32[]{:S(2)}) copy-start(s32[512]{0:T(512)} %param.12) | copy-start | bytes 6148
  4.9 54.1 %all-to-all-start = ((bf16[4,128,4096]{2,1,0:T(8,128)(2,1)}), bf16[4,128,4096]{2,1,0:T(8,128)(2,1)}, u32[]{:S(2)}, u32[]{:S(2)}) async-start(bf16[4,128,4096]{2,1,0:T(8,128)(2,1)} %bitcast.55), calls=%async_computation | async-start | bytes 8388608 | tf_op jit(solution)/shard_map/all_to_all | solution.py:97
  10.1 19.0 %collective-permute-start.4 = (s32[128]{0:T(128)S(1)}, s32[128]{0:T(128)S(1)}, u32[]{:S(2)}, u32[]{:S(2)}) collective-permute-start(s32[128]{0:T(128)S(1)} %slice.56), channel_id=1, source_target_pairs={{4,0},{8,4},{12,8},{16,12},{20,16},{24,20},{28,24},{32,28},{36,32}... | collective-permute-start | bytes 1544 | tf_op jit(solution)/shard_map/ppermute | solution.py:16
  13.9 15.2 %collective-permute-start.3 = (s32[128]{0:T(128)S(1)}, s32[128]{0:T(128)S(1)}, u32[]{:S(2)}, u32[]{:S(2)}) collective-permute-start(s32[128]{0:T(128)S(1)} %slice.54), channel_id=1, source_target_pairs={{0,4},{4,8},{8,12},{12,16},{16,20},{20,24},{24,28},{28,32},{32,36}... | collective-permute-start | bytes 1544 | tf_op jit(solution)/shard_map/ppermute | solution.py:16
  15.9 13.3 %collective-permute-start.1 = (s32[512]{0:T(512)S(1)}, s32[512]{0:T(512)S(1)}, u32[]{:S(2)}, u32[]{:S(2)}) collective-permute-start(s32[512]{0:T(512)S(1)} %copy-done.4), channel_id=1, source_target_pairs={{0,4},{4,8},{8,12},{12,16},{16,20},{20,24},{24,28},{28,32},{32,36}... | collective-permute-start | bytes 6152 | tf_op jit(solution)/shard_map/ppermute | solution.py:16
  29.1 33.0 %copy-start.3 = (f32[4096]{0:T(1024)S(1)}, f32[4096]{0:T(1024)}, u32[]{:S(2)}) copy-start(f32[4096]{0:T(1024)} %param.8) | copy-start | bytes 49156
  67.9 41.0 %collective-permute-start = (bf16[512,256]{1,0:T(8,128)(2,1)S(1)}, bf16[512,256]{1,0:T(8,128)(2,1)}, u32[]{:S(2)}, u32[]{:S(2)}) collective-permute-start(bf16[512,256]{1,0:T(8,128)(2,1)S(1)} %convolution_convert_fusion), channel_id=1, source_target_pairs={{0,4},{4,8},{8,12},{12,16},{16,20},{20,24},{24,28},{28,32},{32,36}... | collective-permute-start | bytes 786440 | tf_op jit(solution)/shard_map/ppermute | solution.py:16
  69.8 4.0 %copy-start.2 = (bf16[256,4096]{1,0:T(8,128)(2,1)S(1)}, bf16[256,4096]{1,0:T(8,128)(2,1)}, u32[]{:S(2)}) copy-start(bf16[256,4096]{1,0:T(8,128)(2,1)} %copy.36) | copy-start | bytes 6291460
  73.8 2.0 %copy-start.1 = (bf16[4,128,4096]{2,1,0:T(8,128)(2,1)}, bf16[4,128,4096]{2,1,0:T(8,128)(2,1)S(1)}, u32[]{:S(2)}) copy-start(bf16[4,128,4096]{2,1,0:T(8,128)(2,1)S(1)} %multiply_convert_fusion) | copy-start | bytes 12582916
  75.8 24.2 %collective-permute-start.8 = (bf16[128,256]{1,0:T(8,128)(2,1)}, bf16[128,256]{1,0:T(8,128)(2,1)}, u32[]{:S(2)}, u32[]{:S(2)}) collective-permute-start(bf16[128,256]{1,0:T(8,128)(2,1)} %get-tuple-element.43), channel_id=1, source_target_pairs={{4,0},{8,4},{12,8},{16,12},{20,16},{24,20},{28,24},{32,28},{36,32}... | collective-permute-start | bytes 196616 | tf_op jit(solution)/shard_map/ppermute | solution.py:16
  82.8 20.2 %collective-permute-start.7 = (bf16[128,256]{1,0:T(8,128)(2,1)}, bf16[128,256]{1,0:T(8,128)(2,1)}, u32[]{:S(2)}, u32[]{:S(2)}) collective-permute-start(bf16[128,256]{1,0:T(8,128)(2,1)} %get-tuple-element.42), channel_id=1, source_target_pairs={{0,4},{4,8},{8,12},{12,16},{16,20},{20,24},{24,28},{28,32},{32,36}... | collective-permute-start | bytes 196616 | tf_op jit(solution)/shard_map/ppermute | solution.py:16
  84.9 24.1 %collective-permute-start.2 = (bf16[512,256]{1,0:T(8,128)(2,1)S(1)}, bf16[512,256]{1,0:T(8,128)(2,1)}, u32[]{:S(2)}, u32[]{:S(2)}) collective-permute-start(bf16[512,256]{1,0:T(8,128)(2,1)S(1)} %copy.37), channel_id=1, source_target_pairs={{0,4},{4,8},{8,12},{12,16},{16,20},{20,24},{24,28},{28,32},{32,36}... | collective-permute-start | bytes 786440 | tf_op jit(solution)/shard_map/ppermute | solution.py:16
  86.9 16.1 %collective-permute-start.6 = (bf16[128,256]{1,0:T(8,128)(2,1)S(1)}, bf16[128,256]{1,0:T(8,128)(2,1)}, u32[]{:S(2)}, u32[]{:S(2)}) collective-permute-start(bf16[128,256]{1,0:T(8,128)(2,1)S(1)} %copy.42), channel_id=1, source_target_pairs={{4,0},{8,4},{12,8},{16,12},{20,16},{24,20},{28,24},{32,28},{36,32}... | collective-permute-start | bytes 196616 | tf_op jit(solution)/shard_map/ppermute | solution.py:16
  100.0 8.9 %collective-permute-start.5 = (bf16[128,256]{1,0:T(8,128)(2,1)S(1)}, bf16[128,256]{1,0:T(8,128)(2,1)S(1)}, u32[]{:S(2)}, u32[]{:S(2)}) collective-permute-start(bf16[128,256]{1,0:T(8,128)(2,1)S(1)} %copy.41), channel_id=1, source_target_pairs={{0,4},{4,8},{8,12},{12,16},{16,20},{20,24},{24,28},{28,32},{32,36}... | collective-permute-start | bytes 196616 | tf_op jit(solution)/shard_map/ppermute | solution.py:16
